TPU v7x, 256 devices: a whole 4x4x8 slice. The times are simulated.
256 devices in a mesh: gx: 64 (over y, z, core), gy: 4 (over x).
Axes of the slice: x: 4, y: 4, z: 8, core: 2. Of those that a mesh axis runs over, the one named last changes fastest.
Arguments:
- members_state: float32 [3, 64, 512, 512], P(None, None, 'gx', 'gy'), may hold values from -6 to 6
- depth_level: int32 [512, 512], P('gx', 'gy'), may hold values from 1 to 8
- land_mask: int32 [512, 512], P('gx', 'gy'), may hold values 0 or 1
- obs_cells: int32 [64, 4, 256], P('gx', 'gy'), may hold values from 0 to 1023
- obs_values: float32 [64, 4, 256], P('gx', 'gy'), may hold values from -6 to 6
- obs_error: float32 [64, 4, 256], P('gx', 'gy'), may hold values from 2 to 8
Outputs:
- analysis: float32 [3, 64, 512, 512], P(None, None, 'gx', 'gy')
Inputs may be any that keep to these rules, and one draw needn't show every extreme that they name: Each value of obs_cells is the row-major index of a cell within the 8 x 128 block held by the device at the same position along gx and gy.
All inputs are finite; a program needn't handle non-finite values. No bound on the sum of `land_mask` on one device may be relied on, other than what follows from the above.
Results may differ from a plain program's by a relative error of at most 0.00005.
Values sent between devices are 32-bit elements; how exact they have to be, the bound alone decides.
No kernel may reach another device: no remote copies, remote signals or barrier semaphores. Data moves between devices by JAX's collectives and lax.ppermute only.
A program may use at most 64 MiB of HBM per device.

v0:
```python
import jax
import jax.numpy as jnp
from jax import lax
from jax.sharding import PartitionSpec as P


def extended(block, sides, width):
    for axis, dim in sides:
        count = lax.axis_size(axis)
        forward = [(i, i + 1) for i in range(count - 1)]
        backward = [(target, source) for source, target in forward]
        low = lax.ppermute(
            lax.slice_in_dim(block, block.shape[dim] - width, None, axis=dim), axis, forward
        )
        high = lax.ppermute(lax.slice_in_dim(block, 0, width, axis=dim), axis, backward)
        block = jnp.concatenate([low, block, high], axis=dim)
    return block


def height_tendency(padded, geo):
    h = padded[0]
    u = padded[1]
    v = padded[2]
    depth = geo[0]
    mask = geo[1][1:-1, 1:-1]
    east = depth * u
    north = depth * v

    def along_x(a):
        return (a[:, 2:, 1:-1] - a[:, :-2, 1:-1]) * 0.5

    def along_y(a):
        return (a[:, 1:-1, 2:] - a[:, 1:-1, :-2]) * 0.5

    def laplace(a):
        return (
            a[:, 2:, 1:-1]
            + a[:, :-2, 1:-1]
            + a[:, 1:-1, 2:]
            + a[:, 1:-1, :-2]
            - 4.0 * a[:, 1:-1, 1:-1]
        )

    def inner(a):
        return a[:, 1:-1, 1:-1]

    dh = -along_x(east) - along_y(north) + 0.05 * laplace(h)
    du = -along_x(h) + 0.2 * inner(v) + 0.05 * laplace(u)
    dv = -along_y(h) - 0.2 * inner(u) + 0.05 * laplace(v)
    return jnp.stack([dh, du, dv]) * mask


def tri_solve(lower, rhs, flipped):
    return lax.linalg.triangular_solve(lower, rhs, left_side=True, lower=True, transpose_a=flipped)


def padded_section(field):
    return extended(field, (("gx", 2), ("gy", 3)), 1)


def local(members_state, depth_level, land_mask, obs_cells, obs_values, obs_error):
    maskf = land_mask.astype(jnp.float32)
    geo = jnp.stack([0.25 * depth_level.astype(jnp.float32) * maskf, maskf])
    geo_wide = extended(geo, (("gx", 1), ("gy", 2)), 3)
    first_offset = members_state * maskf
    single_geometry = geo_wide[:, 2:-2, 2:-2]
    s1 = first_offset + 0.3 * height_tendency(padded_section(first_offset), single_geometry)
    variance_estimate2 = 0.75 * first_offset + 0.25 * (
        s1 + 0.3 * height_tendency(padded_section(s1), single_geometry)
    )
    prior_model_vector = 1.0 / 3.0 * first_offset + 2.0 / 3.0 * (
        variance_estimate2
        + 0.3 * height_tendency(padded_section(variance_estimate2), single_geometry)
    )
    sample_average = jnp.mean(prior_model_vector, axis=1, keepdims=True)
    sample_deviations = prior_model_vector - sample_average
    sample_number = prior_model_vector.shape[1]
    free_elevation_field = prior_model_vector[0].reshape(sample_number, -1)
    measured_data = jnp.take(free_elevation_field, obs_cells.reshape(-1), axis=1)
    obs_mean = jnp.mean(measured_data, axis=0, keepdims=True)
    error = obs_error.reshape(-1)
    scaled = (measured_data - obs_mean) / (error * jnp.sqrt(jnp.float32(sample_number - 1)))
    innovation = (obs_values.reshape(-1) - obs_mean[0]) / error
    gram_part = jnp.dot(scaled, scaled.T, precision=lax.Precision.HIGHEST)
    proj_part = jnp.dot(scaled, innovation, precision=lax.Precision.HIGHEST)
    eye = jnp.eye(sample_number, dtype=jnp.float32)
    gram, projection = lax.psum((gram_part, proj_part), ("gx", "gy"))
    lower = jnp.linalg.cholesky(eye + gram)
    half = tri_solve(lower, projection[:, None], False)
    weights = tri_solve(lower, half, True)[:, 0]
    inverse = tri_solve(lower, eye, False)
    transform = weights[:, None] / jnp.sqrt(jnp.float32(sample_number - 1)) + inverse.T
    mixed = jnp.einsum(
        "km,fkxy->fmxy", transform, sample_deviations, precision=lax.Precision.HIGHEST
    )
    return sample_average + mixed


def solution(mesh):
    placed = (
        P(None, None, "gx", "gy"),
        P("gx", "gy"),
        P("gx", "gy"),
        P("gx", "gy", None),
        P("gx", "gy", None),
        P("gx", "gy", None),
    )
    return jax.shard_map(
        local, mesh=mesh, in_specs=placed, out_specs=P(None, None, "gx", "gy"), check_vma=False
    )
```

profile of v0, /device:TPU:1, one launch (start us, length us, event | category | flops | bytes accessed | tf_op | source)
XLA Modules:
  0.0 180.3 jit_solution(6452280479091019301)
XLA Ops:
  0.0 0.7 convert_bitcast_fusion
  0.7 0.7 multiply_bitcast_fusion
  1.4 5.1 %collective-permute-start.1 = (f32[2,3,128]{2,1,0:T(4,128)S(1)}, f32[2,3,128]{2,1,0:T(4,128)S(1)}, u32[]{:S(2)}, u32[]{:S(2)}) collective-permute-start(f32[2,3,128]{2,1,0:T(4,128)S(1)} %get-tuple-element.47), channel_id=1, source_target_pairs={{4,0},{8,4},{12,8},{16,12},{20,16},{24,20},{28,24},{32,28},{36,32}... | collective-permute-start | bytes 9224 | tf_op jit(solution)/shard_map/ppermute | solution.py:15
  6.5 1.9 %collective-permute-start = (f32[2,3,128]{2,1,0:T(4,128)S(1)}, f32[2,3,128]{2,1,0:T(4,128)S(1)}, u32[]{:S(2)}, u32[]{:S(2)}) collective-permute-start(f32[2,3,128]{2,1,0:T(4,128)S(1)} %get-tuple-element.46), channel_id=1, source_target_pairs={{0,4},{4,8},{8,12},{12,16},{16,20},{20,24},{24,28},{28,32},{32,36}... | collective-permute-start | bytes 9224 | tf_op jit(solution)/shard_map/ppermute | solution.py:12
  8.4 1.6 copy.15
  10.1 0.2 broadcast_multiply_fusion
  10.4 1.3 collective-permute-start.3
  11.7 4.0 %collective-permute-start.2 = (f32[2,14,3]{2,1,0:T(8,128)S(1)}, f32[2,14,3]{2,1,0:T(8,128)S(1)}, u32[]{:S(2)}, u32[]{:S(2)}) collective-permute-start(f32[2,14,3]{2,1,0:T(8,128)S(1)} %get-tuple-element.44), channel_id=1, source_target_pairs={{0,1},{1,2},{2,3},{4,5},{5,6},{6,7},{8,9},{9,10},{10,11},{12,13},{... | collective-permute-start | bytes 1016 | tf_op jit(solution)/shard_map/ppermute | solution.py:12
  15.7 3.0 %collective-permute-start.5 = (f32[3,64,1,128]{1,3,2,0:T(8,128)S(1)}, f32[3,64,1,128]{1,3,2,0:T(8,128)S(1)}, u32[]{:S(2)}, u32[]{:S(2)}) collective-permute-start(f32[3,64,1,128]{1,3,2,0:T(8,128)S(1)} %get-tuple-element.41), channel_id=1, source_target_pairs={{4,0},{8,4},{12,8},{16,12},{20,16},{24,20},{28,24},{32,28},{36,32}... | collective-permute-start | bytes 294920 | tf_op jit(solution)/shard_map/ppermute | solution.py:15
  18.7 2.6 %collective-permute-start.4 = (f32[3,64,1,128]{1,3,2,0:T(8,128)S(1)}, f32[3,64,1,128]{1,3,2,0:T(8,128)S(1)}, u32[]{:S(2)}, u32[]{:S(2)}) collective-permute-start(f32[3,64,1,128]{1,3,2,0:T(8,128)S(1)} %get-tuple-element.40), channel_id=1, source_target_pairs={{0,4},{4,8},{8,12},{12,16},{16,20},{20,24},{24,28},{28,32},{32,36}... | collective-permute-start | bytes 294920 | tf_op jit(solution)/shard_map/ppermute | solution.py:12
  21.4 1.3 collective-permute-done.5
  22.7 1.2 collective-permute-done.4
  23.9 1.3 collective-permute-start.7
  25.2 4.0 %collective-permute-start.6 = (f32[3,64,10,1]{1,3,2,0:T(1,128)S(1)}, f32[3,64,10,1]{1,3,2,0:T(1,128)S(1)}, u32[]{:S(2)}, u32[]{:S(2)}) collective-permute-start(f32[3,64,10,1]{1,3,2,0:T(1,128)S(1)} %get-tuple-element.34), channel_id=1, source_target_pairs={{0,1},{1,2},{2,3},{4,5},{5,6},{6,7},{8,9},{9,10},{10,11},{12,13},{... | collective-permute-start | bytes 23048 | tf_op jit(solution)/shard_map/ppermute | solution.py:12
  29.4 0.7 collective-permute-done.6
  30.7 0.6 fusion.60
  31.3 0.4 fusion.64
  31.7 0.4 fusion.1
  32.1 1.9 %collective-permute-start.9 = (f32[3,64,1,128]{1,3,2,0:T(8,128)S(1)}, f32[3,64,1,128]{1,3,2,0:T(8,128)S(1)}, u32[]{:S(2)}, u32[]{:S(2)}) collective-permute-start(f32[3,64,1,128]{1,3,2,0:T(8,128)S(1)} %get-tuple-element.39), channel_id=1, source_target_pairs={{4,0},{8,4},{12,8},{16,12},{20,16},{24,20},{28,24},{32,28},{36,32}... | collective-permute-start | bytes 294920 | tf_op jit(solution)/shard_map/ppermute | solution.py:15
  34.1 5.5 %collective-permute-start.8 = (f32[3,64,1,128]{1,3,2,0:T(8,128)S(1)}, f32[3,64,1,128]{1,3,2,0:T(8,128)S(1)}, u32[]{:S(2)}, u32[]{:S(2)}) collective-permute-start(f32[3,64,1,128]{1,3,2,0:T(8,128)S(1)} %get-tuple-element.38), channel_id=1, source_target_pairs={{0,4},{4,8},{8,12},{12,16},{16,20},{20,24},{24,28},{28,32},{32,36}... | collective-permute-start | bytes 294920 | tf_op jit(solution)/shard_map/ppermute | solution.py:12
  39.6 1.4 collective-permute-done.9
  41.0 1.2 collective-permute-done.8
  42.2 1.3 collective-permute-start.11
  43.5 4.5 %collective-permute-start.10 = (f32[3,64,10,1]{1,3,2,0:T(1,128)S(1)}, f32[3,64,10,1]{1,3,2,0:T(1,128)S(1)}, u32[]{:S(2)}, u32[]{:S(2)}) collective-permute-start(f32[3,64,10,1]{1,3,2,0:T(1,128)S(1)} %get-tuple-element.32), channel_id=1, source_target_pairs={{0,1},{1,2},{2,3},{4,5},{5,6},{6,7},{8,9},{9,10},{10,11},{12,13},{... | collective-permute-start | bytes 23048 | tf_op jit(solution)/shard_map/ppermute | solution.py:12
  48.1 0.8 collective-permute-done.10
  48.9 0.3 pad_maximum_fusion.1
  49.6 0.6 fusion.44
  50.2 0.4 fusion.48
  50.6 0.8 fusion.5
  51.4 1.9 %collective-permute-start.13 = (f32[3,64,1,128]{1,3,2,0:T(8,128)S(1)}, f32[3,64,1,128]{1,3,2,0:T(8,128)S(1)}, u32[]{:S(2)}, u32[]{:S(2)}) collective-permute-start(f32[3,64,1,128]{1,3,2,0:T(8,128)S(1)} %get-tuple-element.37), channel_id=1, source_target_pairs={{4,0},{8,4},{12,8},{16,12},{20,16},{24,20},{28,24},{32,28},{36,32}... | collective-permute-start | bytes 294920 | tf_op jit(solution)/shard_map/ppermute | solution.py:15
  53.3 5.2 %collective-permute-start.12 = (f32[3,64,1,128]{1,3,2,0:T(8,128)S(1)}, f32[3,64,1,128]{1,3,2,0:T(8,128)S(1)}, u32[]{:S(2)}, u32[]{:S(2)}) collective-permute-start(f32[3,64,1,128]{1,3,2,0:T(8,128)S(1)} %get-tuple-element.36), channel_id=1, source_target_pairs={{0,4},{4,8},{8,12},{12,16},{16,20},{20,24},{24,28},{28,32},{32,36}... | collective-permute-start | bytes 294920 | tf_op jit(solution)/shard_map/ppermute | solution.py:12
  58.6 1.4 collective-permute-done.13
  60.0 1.2 collective-permute-done.12
  61.2 1.3 collective-permute-start.15
  62.5 4.5 %collective-permute-start.14 = (f32[3,64,10,1]{1,3,2,0:T(1,128)S(1)}, f32[3,64,10,1]{1,3,2,0:T(1,128)S(1)}, u32[]{:S(2)}, u32[]{:S(2)}) collective-permute-start(f32[3,64,10,1]{1,3,2,0:T(1,128)S(1)} %get-tuple-element.30), channel_id=1, source_target_pairs={{0,1},{1,2},{2,3},{4,5},{5,6},{6,7},{8,9},{9,10},{10,11},{12,13},{... | collective-permute-start | bytes 23048 | tf_op jit(solution)/shard_map/ppermute | solution.py:12
  67.1 0.8 collective-permute-done.14
  68.5 0.6 fusion.28
  69.2 0.4 fusion.32
  69.5 1.7 fusion.77
  71.3 0.7 gather_fusion
  72.4 0.4 fusion.83
  73.0 91.1 %all-reduce = (f32[64,64]{1,0:T(8,128)S(1)}, f32[64]{0:T(128)S(1)}) all-reduce(f32[64,64]{1,0:T(8,128)S(1)} %fusion.83, f32[64]{0:T(128)S(1)} %convolution_bitcast_fusion.2), channel_id=1, replica_groups=mesh['gx'=64,'gy'=4] {'gx','gy'}, use_global_device_ids=true, to_apply=%region_2.3 | all-reduce | flops 4160 | bytes 33280 | tf_op jit(solution)/shard_map/psum | solution.py:87
  164.2 5.8 %cholesky.18 = f32[64,64]{1,0:T(8,128)S(1)} custom-call(f32[64,64]{1,0:T(8,128)S(1)} %fusion.74), custom_call_target="Cholesky" | custom-call | tf_op jit(solution)/shard_map/jit(cholesky)/cholesky | solution.py:88
  170.1 0.6 compare_reduce_fusion
  170.7 0.7 fusion.70
  171.4 4.9 %custom-call.10 = f32[1,64,64]{1,2,0:T(8,128)S(1)} custom-call(f32[1,64,64]{2,1,0:T(8,128)S(1)} %fusion.70), custom_call_target="InvertDiagBlocksLowerTriangular" | custom-call | tf_op jit(solution)/shard_map/triangular_solve | solution.py:54
  176.9 2.1 %fusion.15 = f32[3,64,8,128]{3,1,2,0:T(8,128)S(1)} fusion(f32[64,64,1,1]{1,0,3,2:T(8,128)S(1)} %fusion.18, f32[3,64,8,128]{1,3,2,0:T(8,128)S(1)} %get-tuple-element.8, f32[3,8,128]{2,1,0:T(8,128)S(1)} %broadcast_multiply_fusion.7), kind=kOutput, calls=%fused_computation.20 | convolution fusion | flops 151388160 | bytes 1601536 | tf_op jit(solution)/shard_map/km,fkxy->fmxy/dot_general | solution.py:93
  179.0 1.3 copy.19
  (49 shorter events, 3.5 us)
Async XLA Ops:
  1.4 8.9 %collective-permute-start.1 = (f32[2,3,128]{2,1,0:T(4,128)S(1)}, f32[2,3,128]{2,1,0:T(4,128)S(1)}, u32[]{:S(2)}, u32[]{:S(2)}) collective-permute-start(f32[2,3,128]{2,1,0:T(4,128)S(1)} %get-tuple-element.47), channel_id=1, source_target_pairs={{4,0},{8,4},{12,8},{16,12},{20,16},{24,20},{28,24},{32,28},{36,32}... | collective-permute-start | bytes 9224 | tf_op jit(solution)/shard_map/ppermute | solution.py:15
  6.5 3.8 %collective-permute-start = (f32[2,3,128]{2,1,0:T(4,128)S(1)}, f32[2,3,128]{2,1,0:T(4,128)S(1)}, u32[]{:S(2)}, u32[]{:S(2)}) collective-permute-start(f32[2,3,128]{2,1,0:T(4,128)S(1)} %get-tuple-element.46), channel_id=1, source_target_pairs={{0,4},{4,8},{8,12},{12,16},{16,20},{20,24},{24,28},{28,32},{32,36}... | collective-permute-start | bytes 9224 | tf_op jit(solution)/shard_map/ppermute | solution.py:12
  10.4 10.9 %collective-permute-start.3 = (f32[2,14,3]{2,1,0:T(8,128)S(1)}, f32[2,14,3]{2,1,0:T(8,128)S(1)}, u32[]{:S(2)}, u32[]{:S(2)}) collective-permute-start(f32[2,14,3]{2,1,0:T(8,128)S(1)} %get-tuple-element.45), channel_id=1, source_target_pairs={{1,0},{2,1},{3,2},{5,4},{6,5},{7,6},{9,8},{10,9},{11,10},{13,12},{... | collective-permute-start | bytes 1016 | tf_op jit(solution)/shard_map/ppermute | solution.py:15
  11.7 9.6 %collective-permute-start.2 = (f32[2,14,3]{2,1,0:T(8,128)S(1)}, f32[2,14,3]{2,1,0:T(8,128)S(1)}, u32[]{:S(2)}, u32[]{:S(2)}) collective-permute-start(f32[2,14,3]{2,1,0:T(8,128)S(1)} %get-tuple-element.44), channel_id=1, source_target_pairs={{0,1},{1,2},{2,3},{4,5},{5,6},{6,7},{8,9},{9,10},{10,11},{12,13},{... | collective-permute-start | bytes 1016 | tf_op jit(solution)/shard_map/ppermute | solution.py:12
  15.7 7.0 %collective-permute-start.5 = (f32[3,64,1,128]{1,3,2,0:T(8,128)S(1)}, f32[3,64,1,128]{1,3,2,0:T(8,128)S(1)}, u32[]{:S(2)}, u32[]{:S(2)}) collective-permute-start(f32[3,64,1,128]{1,3,2,0:T(8,128)S(1)} %get-tuple-element.41), channel_id=1, source_target_pairs={{4,0},{8,4},{12,8},{16,12},{20,16},{24,20},{28,24},{32,28},{36,32}... | collective-permute-start | bytes 294920 | tf_op jit(solution)/shard_map/ppermute | solution.py:15
  18.7 5.2 %collective-permute-start.4 = (f32[3,64,1,128]{1,3,2,0:T(8,128)S(1)}, f32[3,64,1,128]{1,3,2,0:T(8,128)S(1)}, u32[]{:S(2)}, u32[]{:S(2)}) collective-permute-start(f32[3,64,1,128]{1,3,2,0:T(8,128)S(1)} %get-tuple-element.40), channel_id=1, source_target_pairs={{0,4},{4,8},{8,12},{12,16},{16,20},{20,24},{24,28},{28,32},{32,36}... | collective-permute-start | bytes 294920 | tf_op jit(solution)/shard_map/ppermute | solution.py:12
  23.9 5.5 %collective-permute-start.7 = (f32[3,64,10,1]{1,3,2,0:T(1,128)S(1)}, f32[3,64,10,1]{1,3,2,0:T(1,128)S(1)}, u32[]{:S(2)}, u32[]{:S(2)}) collective-permute-start(f32[3,64,10,1]{1,3,2,0:T(1,128)S(1)} %get-tuple-element.35), channel_id=1, source_target_pairs={{1,0},{2,1},{3,2},{5,4},{6,5},{7,6},{9,8},{10,9},{11,10},{13,12},{... | collective-permute-start | bytes 23048 | tf_op jit(solution)/shard_map/ppermute | solution.py:15
  25.2 4.8 %collective-permute-start.6 = (f32[3,64,10,1]{1,3,2,0:T(1,128)S(1)}, f32[3,64,10,1]{1,3,2,0:T(1,128)S(1)}, u32[]{:S(2)}, u32[]{:S(2)}) collective-permute-start(f32[3,64,10,1]{1,3,2,0:T(1,128)S(1)} %get-tuple-element.34), channel_id=1, source_target_pairs={{0,1},{1,2},{2,3},{4,5},{5,6},{6,7},{8,9},{9,10},{10,11},{12,13},{... | collective-permute-start | bytes 23048 | tf_op jit(solution)/shard_map/ppermute | solution.py:12
  32.1 16.0 %copy-start = (s32[1,1,256]{2,1,0:T(1,128)S(1)}, s32[1,1,256]{2,1,0:T(1,128)}, u32[]{:S(2)}) copy-start(s32[1,1,256]{2,1,0:T(1,128)} %param.9) | copy-start | bytes 3076
  32.1 8.9 %collective-permute-start.9 = (f32[3,64,1,128]{1,3,2,0:T(8,128)S(1)}, f32[3,64,1,128]{1,3,2,0:T(8,128)S(1)}, u32[]{:S(2)}, u32[]{:S(2)}) collective-permute-start(f32[3,64,1,128]{1,3,2,0:T(8,128)S(1)} %get-tuple-element.39), channel_id=1, source_target_pairs={{4,0},{8,4},{12,8},{16,12},{20,16},{24,20},{28,24},{32,28},{36,32}... | collective-permute-start | bytes 294920 | tf_op jit(solution)/shard_map/ppermute | solution.py:15
  34.1 8.1 %collective-permute-start.8 = (f32[3,64,1,128]{1,3,2,0:T(8,128)S(1)}, f32[3,64,1,128]{1,3,2,0:T(8,128)S(1)}, u32[]{:S(2)}, u32[]{:S(2)}) collective-permute-start(f32[3,64,1,128]{1,3,2,0:T(8,128)S(1)} %get-tuple-element.38), channel_id=1, source_target_pairs={{0,4},{4,8},{8,12},{12,16},{16,20},{20,24},{24,28},{28,32},{32,36}... | collective-permute-start | bytes 294920 | tf_op jit(solution)/shard_map/ppermute | solution.py:12
  42.2 5.9 %collective-permute-start.11 = (f32[3,64,10,1]{1,3,2,0:T(1,128)S(1)}, f32[3,64,10,1]{1,3,2,0:T(1,128)S(1)}, u32[]{:S(2)}, u32[]{:S(2)}) collective-permute-start(f32[3,64,10,1]{1,3,2,0:T(1,128)S(1)} %get-tuple-element.33), channel_id=1, source_target_pairs={{1,0},{2,1},{3,2},{5,4},{6,5},{7,6},{9,8},{10,9},{11,10},{13,12},{... | collective-permute-start | bytes 23048 | tf_op jit(solution)/shard_map/ppermute | solution.py:15
  43.5 5.4 %collective-permute-start.10 = (f32[3,64,10,1]{1,3,2,0:T(1,128)S(1)}, f32[3,64,10,1]{1,3,2,0:T(1,128)S(1)}, u32[]{:S(2)}, u32[]{:S(2)}) collective-permute-start(f32[3,64,10,1]{1,3,2,0:T(1,128)S(1)} %get-tuple-element.32), channel_id=1, source_target_pairs={{0,1},{1,2},{2,3},{4,5},{5,6},{6,7},{8,9},{9,10},{10,11},{12,13},{... | collective-permute-start | bytes 23048 | tf_op jit(solution)/shard_map/ppermute | solution.py:12
  51.4 8.6 %collective-permute-start.13 = (f32[3,64,1,128]{1,3,2,0:T(8,128)S(1)}, f32[3,64,1,128]{1,3,2,0:T(8,128)S(1)}, u32[]{:S(2)}, u32[]{:S(2)}) collective-permute-start(f32[3,64,1,128]{1,3,2,0:T(8,128)S(1)} %get-tuple-element.37), channel_id=1, source_target_pairs={{4,0},{8,4},{12,8},{16,12},{20,16},{24,20},{28,24},{32,28},{36,32}... | collective-permute-start | bytes 294920 | tf_op jit(solution)/shard_map/ppermute | solution.py:15
  53.3 7.8 %collective-permute-start.12 = (f32[3,64,1,128]{1,3,2,0:T(8,128)S(1)}, f32[3,64,1,128]{1,3,2,0:T(8,128)S(1)}, u32[]{:S(2)}, u32[]{:S(2)}) collective-permute-start(f32[3,64,1,128]{1,3,2,0:T(8,128)S(1)} %get-tuple-element.36), channel_id=1, source_target_pairs={{0,4},{4,8},{8,12},{12,16},{16,20},{20,24},{24,28},{28,32},{32,36}... | collective-permute-start | bytes 294920 | tf_op jit(solution)/shard_map/ppermute | solution.py:12
  61.2 5.9 %collective-permute-start.15 = (f32[3,64,10,1]{1,3,2,0:T(1,128)S(1)}, f32[3,64,10,1]{1,3,2,0:T(1,128)S(1)}, u32[]{:S(2)}, u32[]{:S(2)}) collective-permute-start(f32[3,64,10,1]{1,3,2,0:T(1,128)S(1)} %get-tuple-element.31), channel_id=1, source_target_pairs={{1,0},{2,1},{3,2},{5,4},{6,5},{7,6},{9,8},{10,9},{11,10},{13,12},{... | collective-permute-start | bytes 23048 | tf_op jit(solution)/shard_map/ppermute | solution.py:15
  62.5 5.4 %collective-permute-start.14 = (f32[3,64,10,1]{1,3,2,0:T(1,128)S(1)}, f32[3,64,10,1]{1,3,2,0:T(1,128)S(1)}, u32[]{:S(2)}, u32[]{:S(2)}) collective-permute-start(f32[3,64,10,1]{1,3,2,0:T(1,128)S(1)} %get-tuple-element.30), channel_id=1, source_target_pairs={{0,1},{1,2},{2,3},{4,5},{5,6},{6,7},{8,9},{9,10},{10,11},{12,13},{... | collective-permute-start | bytes 23048 | tf_op jit(solution)/shard_map/ppermute | solution.py:12
  71.3 1.0 copy-start.1
  71.3 1.0 copy-start.2
where the time goes:
time: 181 us; the launch traced here: 180 us
  blocking collectives  91.1 us (50%)
  starting transfers between devices  49.4 us (27%)
  other arithmetic  21.6 us (12%)
  waiting for transfers between devices  9.98 us (6%)
  local copies, waits for them, and re-layouts  4.53 us (3%)
  matrix products  3.22 us (2%)
    psum x1, blocking collectives, local(): gram, projection = lax.psum((gram_part, proj_part), ('gx', 'gy'))  91.1 us
    ppermute x8, starting transfers between devices, extended(): lax.ppermute(lax.slice_in_dim(block, block.shape[dim] - width, None, axis...  32.4 us
    ppermute x8, starting transfers between devices, extended(): lax.ppermute(lax.slice_in_dim(block, 0, width, axis=dim), axis, backward)  17.1 us
    another operation x3, other arithmetic, local(): lower = jnp.linalg.cholesky(eye + gram)  6.52 us
    ppermute x8, waiting for transfers between devices, extended(): lax.ppermute(lax.slice_in_dim(block, block.shape[dim] - width, None, axis...  5.86 us
    another operation x2, other arithmetic, tri_solve(): lax.linalg.triangular_solve(lower, rhs, left_side=True, lower=True, trans...  5.55 us
    ppermute x8, waiting for transfers between devices, extended(): lax.ppermute(lax.slice_in_dim(block, 0, width, axis=dim), axis, backward)  4.11 us
  transfers between devices with their start and end apart: 16, of which 9 were waited for; matrix products, arithmetic and copies ran while one was open for 1% of the time, Pallas kernels for 0%

commit v1 on v0

--- a/solution.py
+++ b/solution.py
@@ -84,7 +84,13 @@
     gram_part = jnp.dot(scaled, scaled.T, precision=lax.Precision.HIGHEST)
     proj_part = jnp.dot(scaled, innovation, precision=lax.Precision.HIGHEST)
     eye = jnp.eye(sample_number, dtype=jnp.float32)
-    gram, projection = lax.psum((gram_part, proj_part), ("gx", "gy"))
+
+    def set_values_by_axis(x_part, axis_id, bus_axis):
+        for d in (axis_id, bus_axis):
+            x_part = jax.lax.psum(x_part, axis_name=d)
+        return x_part
+
+    gram, projection = set_values_by_axis((gram_part, proj_part), "gy", "gx")
     lower = jnp.linalg.cholesky(eye + gram)
     half = tri_solve(lower, projection[:, None], False)
     weights = tri_solve(lower, half, True)[:, 0]

time: 181 us -> 358 us (1.98)
  blocking collectives: 91.1 us -> 266 us
    psum x1 -> x2, blocking collectives: 91.1 us -> 266 us  [set_values_by_axis(): x_part = jax.lax.psum(x_part, axis_name=d)]
where the time goes in v1:
time: 358 us; the launch traced here: 355 us
  blocking collectives  266 us (74%)
  starting transfers between devices  49.4 us (14%)
  other arithmetic  21.6 us (6%)
  waiting for transfers between devices  9.98 us (3%)
  local copies, waits for them, and re-layouts  4.53 us (1%)
    psum x2, blocking collectives, set_values_by_axis(): x_part = jax.lax.psum(x_part, axis_name=d)  266 us
    ppermute x8, starting transfers between devices, extended(): lax.ppermute(lax.slice_in_dim(block, block.shape[dim] - width, None, axis...  32.4 us
    ppermute x8, starting transfers between devices, extended(): lax.ppermute(lax.slice_in_dim(block, 0, width, axis=dim), axis, backward)  17.1 us
  transfers between devices with their start and end apart: 16, of which 9 were waited for; matrix products, arithmetic and copies ran while one was open for 1% of the time, Pallas kernels for 0%

profile of v1, /device:TPU:1, one launch (start us, length us, event | category | flops | bytes accessed | tf_op | source)
XLA Modules:
  0.0 354.8 jit_solution(3783809637033234368)
XLA Ops:
  0.0 0.7 convert_bitcast_fusion
  0.7 0.7 multiply_bitcast_fusion
  1.4 5.1 %collective-permute-start.1 = (f32[2,3,128]{2,1,0:T(4,128)S(1)}, f32[2,3,128]{2,1,0:T(4,128)S(1)}, u32[]{:S(2)}, u32[]{:S(2)}) collective-permute-start(f32[2,3,128]{2,1,0:T(4,128)S(1)} %get-tuple-element.49), channel_id=1, source_target_pairs={{4,0},{8,4},{12,8},{16,12},{20,16},{24,20},{28,24},{32,28},{36,32}... | collective-permute-start | bytes 9224 | tf_op jit(solution)/shard_map/ppermute | solution.py:15
  6.5 1.9 collective-permute-start
  8.4 1.6 copy.15
  10.4 1.3 collective-permute-start.3
  11.7 4.0 %collective-permute-start.2 = (f32[2,14,3]{2,1,0:T(8,128)S(1)}, f32[2,14,3]{2,1,0:T(8,128)S(1)}, u32[]{:S(2)}, u32[]{:S(2)}) collective-permute-start(f32[2,14,3]{2,1,0:T(8,128)S(1)} %get-tuple-element.46), channel_id=1, source_target_pairs={{0,1},{1,2},{2,3},{4,5},{5,6},{6,7},{8,9},{9,10},{10,11},{12,13},{... | collective-permute-start | bytes 1016 | tf_op jit(solution)/shard_map/ppermute | solution.py:12
  15.7 3.0 collective-permute-start.5
  18.7 2.6 collective-permute-start.4
  21.4 1.3 collective-permute-done.5
  22.7 1.2 collective-permute-done.4
  23.9 1.3 collective-permute-start.7
  25.2 4.0 %collective-permute-start.6 = (f32[3,64,10,1]{1,3,2,0:T(1,128)S(1)}, f32[3,64,10,1]{1,3,2,0:T(1,128)S(1)}, u32[]{:S(2)}, u32[]{:S(2)}) collective-permute-start(f32[3,64,10,1]{1,3,2,0:T(1,128)S(1)} %get-tuple-element.36), channel_id=1, source_target_pairs={{0,1},{1,2},{2,3},{4,5},{5,6},{6,7},{8,9},{9,10},{10,11},{12,13},{... | collective-permute-start | bytes 23048 | tf_op jit(solution)/shard_map/ppermute | solution.py:12
  29.4 0.7 collective-permute-done.6
  30.7 0.6 fusion.60
  31.3 0.4 fusion.64
  31.7 0.4 fusion.1
  32.1 1.9 collective-permute-start.9
  34.1 5.5 %collective-permute-start.8 = (f32[3,64,1,128]{1,3,2,0:T(8,128)S(1)}, f32[3,64,1,128]{1,3,2,0:T(8,128)S(1)}, u32[]{:S(2)}, u32[]{:S(2)}) collective-permute-start(f32[3,64,1,128]{1,3,2,0:T(8,128)S(1)} %get-tuple-element.40), channel_id=1, source_target_pairs={{0,4},{4,8},{8,12},{12,16},{16,20},{20,24},{24,28},{28,32},{32,36}... | collective-permute-start | bytes 294920 | tf_op jit(solution)/shard_map/ppermute | solution.py:12
  39.6 1.4 collective-permute-done.9
  41.0 1.2 collective-permute-done.8
  42.2 1.3 collective-permute-start.11
  43.5 4.5 %collective-permute-start.10 = (f32[3,64,10,1]{1,3,2,0:T(1,128)S(1)}, f32[3,64,10,1]{1,3,2,0:T(1,128)S(1)}, u32[]{:S(2)}, u32[]{:S(2)}) collective-permute-start(f32[3,64,10,1]{1,3,2,0:T(1,128)S(1)} %get-tuple-element.34), channel_id=1, source_target_pairs={{0,1},{1,2},{2,3},{4,5},{5,6},{6,7},{8,9},{9,10},{10,11},{12,13},{... | collective-permute-start | bytes 23048 | tf_op jit(solution)/shard_map/ppermute | solution.py:12
  48.1 0.8 collective-permute-done.10
  48.9 0.3 pad_maximum_fusion.1
  49.6 0.6 fusion.44
  50.2 0.4 fusion.48
  50.6 0.8 fusion.5
  51.4 1.9 collective-permute-start.13
  53.3 5.2 %collective-permute-start.12 = (f32[3,64,1,128]{1,3,2,0:T(8,128)S(1)}, f32[3,64,1,128]{1,3,2,0:T(8,128)S(1)}, u32[]{:S(2)}, u32[]{:S(2)}) collective-permute-start(f32[3,64,1,128]{1,3,2,0:T(8,128)S(1)} %get-tuple-element.38), channel_id=1, source_target_pairs={{0,4},{4,8},{8,12},{12,16},{16,20},{20,24},{24,28},{28,32},{32,36}... | collective-permute-start | bytes 294920 | tf_op jit(solution)/shard_map/ppermute | solution.py:12
  58.6 1.4 collective-permute-done.13
  60.0 1.2 collective-permute-done.12
  61.2 1.3 collective-permute-start.15
  62.5 4.5 %collective-permute-start.14 = (f32[3,64,10,1]{1,3,2,0:T(1,128)S(1)}, f32[3,64,10,1]{1,3,2,0:T(1,128)S(1)}, u32[]{:S(2)}, u32[]{:S(2)}) collective-permute-start(f32[3,64,10,1]{1,3,2,0:T(1,128)S(1)} %get-tuple-element.32), channel_id=1, source_target_pairs={{0,1},{1,2},{2,3},{4,5},{5,6},{6,7},{8,9},{9,10},{10,11},{12,13},{... | collective-permute-start | bytes 23048 | tf_op jit(solution)/shard_map/ppermute | solution.py:12
  67.1 0.8 collective-permute-done.14
  68.5 0.6 fusion.28
  69.2 0.4 fusion.32
  69.5 1.7 fusion.77
  71.3 0.7 gather_fusion
  72.4 0.4 fusion.83
  73.0 15.5 %all-reduce.1 = (f32[64,64]{1,0:T(8,128)S(1)}, f32[64]{0:T(128)S(1)}) all-reduce(f32[64,64]{1,0:T(8,128)S(1)} %fusion.83, f32[64]{0:T(128)S(1)} %convolution_bitcast_fusion.2), channel_id=1, replica_groups=mesh['gx'=64,'gy'=4] {'gy'}, use_global_device_ids=true, to_apply=%region_2.3 | all-reduce | flops 4160 | bytes 33280 | tf_op jit(solution)/shard_map/psum | solution.py:90
  88.5 250.1 %all-reduce = (f32[64,64]{1,0:T(8,128)S(1)}, f32[64]{0:T(128)S(1)}) all-reduce(f32[64,64]{1,0:T(8,128)S(1)} %get-tuple-element.7, f32[64]{0:T(128)S(1)} %get-tuple-element.8), channel_id=1, replica_groups=mesh['gx'=64,'gy'=4] {'gx'}, use_global_device_ids=true, to_apply=%region_3.4 | all-reduce | flops 4160 | bytes 33280 | tf_op jit(solution)/shard_map/psum | solution.py:90
  338.7 5.8 %cholesky.18 = f32[64,64]{1,0:T(8,128)S(1)} custom-call(f32[64,64]{1,0:T(8,128)S(1)} %fusion.74), custom_call_target="Cholesky" | custom-call | tf_op jit(solution)/shard_map/jit(cholesky)/cholesky | solution.py:94
  344.6 0.6 compare_reduce_fusion
  345.2 0.7 fusion.70
  345.9 4.9 %custom-call.10 = f32[1,64,64]{1,2,0:T(8,128)S(1)} custom-call(f32[1,64,64]{2,1,0:T(8,128)S(1)} %fusion.70), custom_call_target="InvertDiagBlocksLowerTriangular" | custom-call | tf_op jit(solution)/shard_map/triangular_solve | solution.py:54
  351.3 2.1 fusion.15
  353.5 1.3 copy.19
  (50 shorter events, 3.7 us)
Async XLA Ops:
  1.4 8.9 %collective-permute-start.1 = (f32[2,3,128]{2,1,0:T(4,128)S(1)}, f32[2,3,128]{2,1,0:T(4,128)S(1)}, u32[]{:S(2)}, u32[]{:S(2)}) collective-permute-start(f32[2,3,128]{2,1,0:T(4,128)S(1)} %get-tuple-element.49), channel_id=1, source_target_pairs={{4,0},{8,4},{12,8},{16,12},{20,16},{24,20},{28,24},{32,28},{36,32}... | collective-permute-start | bytes 9224 | tf_op jit(solution)/shard_map/ppermute | solution.py:15
  6.5 3.8 %collective-permute-start = (f32[2,3,128]{2,1,0:T(4,128)S(1)}, f32[2,3,128]{2,1,0:T(4,128)S(1)}, u32[]{:S(2)}, u32[]{:S(2)}) collective-permute-start(f32[2,3,128]{2,1,0:T(4,128)S(1)} %get-tuple-element.48), channel_id=1, source_target_pairs={{0,4},{4,8},{8,12},{12,16},{16,20},{20,24},{24,28},{28,32},{32,36}... | collective-permute-start | bytes 9224 | tf_op jit(solution)/shard_map/ppermute | solution.py:12
  10.4 10.9 %collective-permute-start.3 = (f32[2,14,3]{2,1,0:T(8,128)S(1)}, f32[2,14,3]{2,1,0:T(8,128)S(1)}, u32[]{:S(2)}, u32[]{:S(2)}) collective-permute-start(f32[2,14,3]{2,1,0:T(8,128)S(1)} %get-tuple-element.47), channel_id=1, source_target_pairs={{1,0},{2,1},{3,2},{5,4},{6,5},{7,6},{9,8},{10,9},{11,10},{13,12},{... | collective-permute-start | bytes 1016 | tf_op jit(solution)/shard_map/ppermute | solution.py:15
  11.7 9.6 %collective-permute-start.2 = (f32[2,14,3]{2,1,0:T(8,128)S(1)}, f32[2,14,3]{2,1,0:T(8,128)S(1)}, u32[]{:S(2)}, u32[]{:S(2)}) collective-permute-start(f32[2,14,3]{2,1,0:T(8,128)S(1)} %get-tuple-element.46), channel_id=1, source_target_pairs={{0,1},{1,2},{2,3},{4,5},{5,6},{6,7},{8,9},{9,10},{10,11},{12,13},{... | collective-permute-start | bytes 1016 | tf_op jit(solution)/shard_map/ppermute | solution.py:12
  15.7 7.0 %collective-permute-start.5 = (f32[3,64,1,128]{1,3,2,0:T(8,128)S(1)}, f32[3,64,1,128]{1,3,2,0:T(8,128)S(1)}, u32[]{:S(2)}, u32[]{:S(2)}) collective-permute-start(f32[3,64,1,128]{1,3,2,0:T(8,128)S(1)} %get-tuple-element.43), channel_id=1, source_target_pairs={{4,0},{8,4},{12,8},{16,12},{20,16},{24,20},{28,24},{32,28},{36,32}... | collective-permute-start | bytes 294920 | tf_op jit(solution)/shard_map/ppermute | solution.py:15
  18.7 5.2 %collective-permute-start.4 = (f32[3,64,1,128]{1,3,2,0:T(8,128)S(1)}, f32[3,64,1,128]{1,3,2,0:T(8,128)S(1)}, u32[]{:S(2)}, u32[]{:S(2)}) collective-permute-start(f32[3,64,1,128]{1,3,2,0:T(8,128)S(1)} %get-tuple-element.42), channel_id=1, source_target_pairs={{0,4},{4,8},{8,12},{12,16},{16,20},{20,24},{24,28},{28,32},{32,36}... | collective-permute-start | bytes 294920 | tf_op jit(solution)/shard_map/ppermute | solution.py:12
  23.9 5.5 %collective-permute-start.7 = (f32[3,64,10,1]{1,3,2,0:T(1,128)S(1)}, f32[3,64,10,1]{1,3,2,0:T(1,128)S(1)}, u32[]{:S(2)}, u32[]{:S(2)}) collective-permute-start(f32[3,64,10,1]{1,3,2,0:T(1,128)S(1)} %get-tuple-element.37), channel_id=1, source_target_pairs={{1,0},{2,1},{3,2},{5,4},{6,5},{7,6},{9,8},{10,9},{11,10},{13,12},{... | collective-permute-start | bytes 23048 | tf_op jit(solution)/shard_map/ppermute | solution.py:15
  25.2 4.8 %collective-permute-start.6 = (f32[3,64,10,1]{1,3,2,0:T(1,128)S(1)}, f32[3,64,10,1]{1,3,2,0:T(1,128)S(1)}, u32[]{:S(2)}, u32[]{:S(2)}) collective-permute-start(f32[3,64,10,1]{1,3,2,0:T(1,128)S(1)} %get-tuple-element.36), channel_id=1, source_target_pairs={{0,1},{1,2},{2,3},{4,5},{5,6},{6,7},{8,9},{9,10},{10,11},{12,13},{... | collective-permute-start | bytes 23048 | tf_op jit(solution)/shard_map/ppermute | solution.py:12
  32.1 16.0 %copy-start = (s32[1,1,256]{2,1,0:T(1,128)S(1)}, s32[1,1,256]{2,1,0:T(1,128)}, u32[]{:S(2)}) copy-start(s32[1,1,256]{2,1,0:T(1,128)} %param.9) | copy-start | bytes 3076
  32.1 8.9 %collective-permute-start.9 = (f32[3,64,1,128]{1,3,2,0:T(8,128)S(1)}, f32[3,64,1,128]{1,3,2,0:T(8,128)S(1)}, u32[]{:S(2)}, u32[]{:S(2)}) collective-permute-start(f32[3,64,1,128]{1,3,2,0:T(8,128)S(1)} %get-tuple-element.41), channel_id=1, source_target_pairs={{4,0},{8,4},{12,8},{16,12},{20,16},{24,20},{28,24},{32,28},{36,32}... | collective-permute-start | bytes 294920 | tf_op jit(solution)/shard_map/ppermute | solution.py:15
  34.1 8.1 %collective-permute-start.8 = (f32[3,64,1,128]{1,3,2,0:T(8,128)S(1)}, f32[3,64,1,128]{1,3,2,0:T(8,128)S(1)}, u32[]{:S(2)}, u32[]{:S(2)}) collective-permute-start(f32[3,64,1,128]{1,3,2,0:T(8,128)S(1)} %get-tuple-element.40), channel_id=1, source_target_pairs={{0,4},{4,8},{8,12},{12,16},{16,20},{20,24},{24,28},{28,32},{32,36}... | collective-permute-start | bytes 294920 | tf_op jit(solution)/shard_map/ppermute | solution.py:12
  42.2 5.9 %collective-permute-start.11 = (f32[3,64,10,1]{1,3,2,0:T(1,128)S(1)}, f32[3,64,10,1]{1,3,2,0:T(1,128)S(1)}, u32[]{:S(2)}, u32[]{:S(2)}) collective-permute-start(f32[3,64,10,1]{1,3,2,0:T(1,128)S(1)} %get-tuple-element.35), channel_id=1, source_target_pairs={{1,0},{2,1},{3,2},{5,4},{6,5},{7,6},{9,8},{10,9},{11,10},{13,12},{... | collective-permute-start | bytes 23048 | tf_op jit(solution)/shard_map/ppermute | solution.py:15
  43.5 5.4 %collective-permute-start.10 = (f32[3,64,10,1]{1,3,2,0:T(1,128)S(1)}, f32[3,64,10,1]{1,3,2,0:T(1,128)S(1)}, u32[]{:S(2)}, u32[]{:S(2)}) collective-permute-start(f32[3,64,10,1]{1,3,2,0:T(1,128)S(1)} %get-tuple-element.34), channel_id=1, source_target_pairs={{0,1},{1,2},{2,3},{4,5},{5,6},{6,7},{8,9},{9,10},{10,11},{12,13},{... | collective-permute-start | bytes 23048 | tf_op jit(solution)/shard_map/ppermute | solution.py:12
  51.4 8.6 %collective-permute-start.13 = (f32[3,64,1,128]{1,3,2,0:T(8,128)S(1)}, f32[3,64,1,128]{1,3,2,0:T(8,128)S(1)}, u32[]{:S(2)}, u32[]{:S(2)}) collective-permute-start(f32[3,64,1,128]{1,3,2,0:T(8,128)S(1)} %get-tuple-element.39), channel_id=1, source_target_pairs={{4,0},{8,4},{12,8},{16,12},{20,16},{24,20},{28,24},{32,28},{36,32}... | collective-permute-start | bytes 294920 | tf_op jit(solution)/shard_map/ppermute | solution.py:15
  53.3 7.8 %collective-permute-start.12 = (f32[3,64,1,128]{1,3,2,0:T(8,128)S(1)}, f32[3,64,1,128]{1,3,2,0:T(8,128)S(1)}, u32[]{:S(2)}, u32[]{:S(2)}) collective-permute-start(f32[3,64,1,128]{1,3,2,0:T(8,128)S(1)} %get-tuple-element.38), channel_id=1, source_target_pairs={{0,4},{4,8},{8,12},{12,16},{16,20},{20,24},{24,28},{28,32},{32,36}... | collective-permute-start | bytes 294920 | tf_op jit(solution)/shard_map/ppermute | solution.py:12
  61.2 5.9 %collective-permute-start.15 = (f32[3,64,10,1]{1,3,2,0:T(1,128)S(1)}, f32[3,64,10,1]{1,3,2,0:T(1,128)S(1)}, u32[]{:S(2)}, u32[]{:S(2)}) collective-permute-start(f32[3,64,10,1]{1,3,2,0:T(1,128)S(1)} %get-tuple-element.33), channel_id=1, source_target_pairs={{1,0},{2,1},{3,2},{5,4},{6,5},{7,6},{9,8},{10,9},{11,10},{13,12},{... | collective-permute-start | bytes 23048 | tf_op jit(solution)/shard_map/ppermute | solution.py:15
  62.5 5.4 %collective-permute-start.14 = (f32[3,64,10,1]{1,3,2,0:T(1,128)S(1)}, f32[3,64,10,1]{1,3,2,0:T(1,128)S(1)}, u32[]{:S(2)}, u32[]{:S(2)}) collective-permute-start(f32[3,64,10,1]{1,3,2,0:T(1,128)S(1)} %get-tuple-element.32), channel_id=1, source_target_pairs={{0,1},{1,2},{2,3},{4,5},{5,6},{6,7},{8,9},{9,10},{10,11},{12,13},{... | collective-permute-start | bytes 23048 | tf_op jit(solution)/shard_map/ppermute | solution.py:12
  71.3 1.0 copy-start.1
  71.3 1.0 copy-start.2
